TPU v7x, 256 devices: a whole 4x4x8 slice. The times are simulated.
256 devices in a mesh: occ: 64 (over x_hi, y, z), off: 4 (over x_lo, core).
Axes of the slice: x: 4 (x_hi: 2, x_lo: 2; x = x_hi * 2 + x_lo), y: 4, z: 8, core: 2. Of those that a mesh axis runs over, the one named last changes fastest.
Arguments:
- factors: bfloat16 [64, 768, 2048], P('occ'), may hold values from -0.8984375 to 0.8984375
- occ_level: int32 [64], replicated, may hold values from 0 to 255
- vir_level: int32 [768], replicated, may hold values from 0 to 255
- occupied_energy_levels: float32 [256], replicated, may hold values from -2 to -0.5
- vir_table: float32 [256], replicated, may hold values from 0.5 to 4
- virtual_coefficient_matrix: bfloat16 [768, 1024], replicated, may hold values from -0.21875 to 0.21875
Outputs:
- density_ao: float32 [64, 2048, 1024], P(None, ('occ', 'off'))
Inputs may be any that keep to these rules, and one draw needn't show every extreme that they name: `occ_level`: indices into occupied_energy_levels. `vir_level`: indices into vir_table.
All inputs are finite; a program needn't handle non-finite values.
Results may differ from a plain program's by a relative error of at most 0.0032.
Values may be sent and summed in bfloat16 or wider, within the bound.
No kernel may reach another device: no remote copies, remote signals or barrier semaphores. Data moves between devices by JAX's collectives and lax.ppermute only.
A program may use at most 64 MiB of HBM per device.

v0:
```python
import jax
import jax.numpy as jnp
from jax import lax
from jax.sharding import PartitionSpec as P

PAIR_STEPS = 2


def passed_along(value, axis, by):
    length = lax.axis_size(axis)
    return lax.ppermute(value, axis, [(i, (i + by) % length) for i in range(length)])


def lookup(level, table):
    hits = level[:, None] == jnp.arange(table.shape[0], dtype=jnp.int32)[None, :]
    return jnp.sum(jnp.where(hits, table[None, :], jnp.float32(0.0)), axis=1)


def body(
    factors, occ_level, vir_level, occupied_energy_levels, vir_table, virtual_coefficient_matrix
):
    off_count = lax.axis_size("off")
    off_index = lax.axis_index("off")
    occ_count = lax.axis_size("occ")
    occ_index = lax.axis_index("occ")
    vir_energy = lookup(vir_level, vir_table)
    occ_energy = lookup(occ_level, occupied_energy_levels)
    own_energy = lax.dynamic_index_in_dim(occ_energy, occ_index, 0, keepdims=False)
    own = factors[0]
    carried = factors
    moved = factors
    for stride in range(1, off_count):
        moved = passed_along(moved, "occ", 1)
        carried = jnp.where(off_index == stride, moved, carried)
    gamma = jnp.zeros((own.shape[1], own.shape[0]), jnp.float32)
    for step_index in range(PAIR_STEPS):
        offset = off_index + off_count * step_index
        pair_companion = (occ_index - offset) % occ_count
        other_energy = lax.dynamic_index_in_dim(occ_energy, pair_companion, 0, keepdims=False)
        other = carried[0]
        if step_index < PAIR_STEPS - 1:
            carried = passed_along(carried, "occ", off_count)
        integral = lax.dot_general(
            own, other, (((1,), (1,)), ((), ())), preferred_element_type=jnp.float32
        )
        denom = vir_energy[:, None] + vir_energy[None, :] - own_energy - other_energy
        amp = integral / denom
        pair_weight = (2.0 * amp - amp.T).astype(jnp.bfloat16)
        gamma = gamma + lax.dot_general(
            other, pair_weight, (((0,), (1,)), ((), ())), preferred_element_type=jnp.float32
        )
    naux_rows = gamma.shape[0]
    per_device = naux_rows // (occ_count * off_count)
    blocks = gamma.reshape(occ_count, off_count, per_device, gamma.shape[1])
    total = lax.psum(blocks, "off")
    mine = lax.dynamic_slice_in_dim(total, off_index, 1, 1)
    lower_gamma_part = mine.reshape(occ_count, per_device, gamma.shape[1]).astype(jnp.bfloat16)
    finished_flag = jnp.einsum(
        "sbd,dw->sbw",
        lower_gamma_part,
        virtual_coefficient_matrix,
        preferred_element_type=jnp.float32,
    )
    moved_back = lax.all_to_all(finished_flag[None], "occ", split_axis=1, concat_axis=0, tiled=True)
    return moved_back.reshape(moved_back.shape[0], per_device, virtual_coefficient_matrix.shape[1])


def solution(mesh):
    in_specs = (P("occ", None, None), P(), P(), P(), P(), P())
    out_specs = P(None, ("occ", "off"), None)
    return jax.shard_map(body, mesh=mesh, in_specs=in_specs, out_specs=out_specs, check_vma=False)
```

profile of v0, /device:TPU:56, one launch (start us, length us, event | category | flops | bytes accessed | tf_op | source)
XLA Modules:
  0.0 574.3 jit_solution(9931685049981466083)
XLA Ops:
  0.0 0.0 copy-start
  0.0 1.9 collective-permute-start
  1.9 68.1 %collective-permute-done = bf16[1,768,2048]{2,1,0:T(8,128)(2,1)S(1)} collective-permute-done((bf16[1,768,2048]{2,1,0:T(8,128)(2,1)}, bf16[1,768,2048]{2,1,0:T(8,128)(2,1)S(1)}, u32[]{:S(2)}, u32[]{:S(2)}) %collective-permute-start) | collective-permute-done | bytes 3145760 | tf_op jit(solution)/shard_map/ppermute | solution.py:11
  70.1 1.6 copy-done.1
  71.7 1.9 collective-permute-start.1
  73.6 70.1 %collective-permute-done.1 = bf16[1,768,2048]{2,1,0:T(8,128)(2,1)} collective-permute-done((bf16[1,768,2048]{2,1,0:T(8,128)(2,1)S(1)}, bf16[1,768,2048]{2,1,0:T(8,128)(2,1)}, u32[]{:S(2)}, u32[]{:S(2)}) %collective-permute-start.1) | collective-permute-done | bytes 3145760 | tf_op jit(solution)/shard_map/ppermute | solution.py:11
  143.7 0.0 collective-permute-start.2
  143.7 0.0 copy-start.5
  143.7 70.8 %collective-permute-done.2 = bf16[1,768,2048]{2,1,0:T(8,128)(2,1)} collective-permute-done((bf16[1,768,2048]{2,1,0:T(8,128)(2,1)}, bf16[1,768,2048]{2,1,0:T(8,128)(2,1)}, u32[]{:S(2)}, u32[]{:S(2)}) %collective-permute-start.2) | collective-permute-done | bytes 3145760 | tf_op jit(solution)/shard_map/ppermute | solution.py:11
  214.5 4.1 select_select_fusion
  218.6 2.6 collective-permute-start.3
  221.3 0.0 copy-done.6
  221.3 0.0 copy-done.7
  221.3 0.2 select_reduce_fusion.1
  221.5 0.7 fusion.33
  222.1 0.0 copy-done.4
  222.1 0.0 copy-done.5
  222.1 0.3 select_reduce_fusion
  222.4 6.9 %fusion.5 = f32[768,768]{1,0:T(8,128)} fusion(bf16[1,768,2048]{2,1,0:T(8,128)(2,1)} %param.6, bf16[1,768,2048]{2,1,0:T(8,128)(2,1)} %select_select_fusion), kind=kOutput, calls=%fused_computation.6 | convolution fusion | flops 2415919104 | bytes 8650752 | tf_op jit(solution)/shard_map/dot_general | solution.py:43
  229.3 3.1 copy.14
  232.5 126.0 %collective-permute-done.3 = bf16[1,768,2048]{2,1,0:T(8,128)(2,1)} collective-permute-done((bf16[1,768,2048]{2,1,0:T(8,128)(2,1)}, bf16[1,768,2048]{2,1,0:T(8,128)(2,1)}, u32[]{:S(2)}, u32[]{:S(2)}) %collective-permute-start.3) | collective-permute-done | bytes 3145760 | tf_op jit(solution)/shard_map/ppermute | solution.py:11
  358.4 7.0 %fusion.2 = f32[768,768]{1,0:T(8,128)} fusion(bf16[1,768,2048]{2,1,0:T(8,128)(2,1)} %collective-permute-done.3, bf16[1,768,2048]{2,1,0:T(8,128)(2,1)} %param.6), kind=kOutput, calls=%fused_computation.3 | convolution fusion | flops 2415919104 | bytes 8650752 | tf_op jit(solution)/shard_map/dot_general | solution.py:43
  365.4 3.1 copy.15
  368.5 8.3 %fusion = f32[2048,768]{1,0:T(8,128)S(1)} fusion(bf16[1,768,2048]{2,1,0:T(8,128)(2,1)} %collective-permute-done.3, f32[768,768]{0,1:T(8,128)} %copy.15, f32[768,768]{1,0:T(8,128)} %fusion.2, f32[]{:T(128)} %bitcast.7, f32[]{:T(128)} %bitcast.3, f32[768]{0:T(1024)S(1)} %select_reduce_fusion), kind=kOutput, calls=%fused_computation.1 | convolution fusion | flops 2420637696 | bytes 14158856 | tf_op jit(solution)/shard_map/dot_general | solution.py:49
  376.8 0.0 copy-done.2
  376.8 0.0 copy-done.3
  376.8 6.7 %convolution_add_fusion = f32[2048,768]{1,0:T(8,128)S(1)} fusion(f32[2048,768]{1,0:T(8,128)S(1)} %fusion, bf16[1,768,2048]{2,1,0:T(8,128)(2,1)} %select_select_fusion, f32[768,768]{0,1:T(8,128)S(1)} %copy-done.3, f32[768,768]{1,0:T(8,128)S(1)} %copy-done.2, f32[]{:T(128)} %bitcast.4, f32[]{:T(128)} %bitcast.3, f32[768]{0:T(1024)S(1)} %select_reduce_fusion), kind=kOutput, calls=%fused_computation | convolution fusion | flops 2422210560 | bytes 20450312 | tf_op jit(solution)/shard_map/dot_general | solution.py:49
  383.5 3.2 copy.16
  386.7 111.8 %all-reduce.1 = bf16[64,4,8,768]{3,2,0,1:T(8,128)(2,1)} all-reduce(f32[64,4,8,768]{3,2,0,1:T(8,128)} %copy.16), channel_id=1, replica_groups=mesh['occ'=64,'off'=4] {'off'}, use_global_device_ids=true, to_apply=%region_2.3 | all-reduce | flops 1572864 | bytes 9437184 | tf_op jit(solution)/shard_map/psum | solution.py:55
  498.6 2.1 convolution_bitcast_fusion
  500.7 72.3 %all_to_all.4 = f32[1,64,8,1024]{3,2,0,1:T(8,128)S(1)} all-to-all(f32[1,64,8,1024]{3,2,0,1:T(8,128)S(1)} %convolution_bitcast_fusion), channel_id=1, replica_groups=mesh['occ'=64,'off'=4] {'occ'}, dimensions={1} | all-to-all | bytes 4194304 | tf_op jit(solution)/shard_map/all_to_all | solution.py:64
  572.9 1.3 copy.21
  (7 shorter events, 0.0 us)
Async XLA Ops:
  0.0 498.6 %copy-start = (bf16[768,1024]{1,0:T(8,128)(2,1)S(1)}, bf16[768,1024]{1,0:T(8,128)(2,1)}, u32[]{:S(2)}) copy-start(bf16[768,1024]{1,0:T(8,128)(2,1)} %param.11) | copy-start | bytes 4718596
  0.0 70.1 %collective-permute-start = (bf16[1,768,2048]{2,1,0:T(8,128)(2,1)}, bf16[1,768,2048]{2,1,0:T(8,128)(2,1)S(1)}, u32[]{:S(2)}, u32[]{:S(2)}) collective-permute-start(bf16[1,768,2048]{2,1,0:T(8,128)(2,1)} %param.6), channel_id=1, source_target_pairs={{0,4},{4,8},{8,12},{12,16},{16,20},{20,24},{24,28},{28,32},{32,36}... | collective-permute-start | bytes 9437192 | tf_op jit(solution)/shard_map/ppermute | solution.py:11
  70.1 1.6 copy-start.1
  71.7 72.0 %collective-permute-start.1 = (bf16[1,768,2048]{2,1,0:T(8,128)(2,1)S(1)}, bf16[1,768,2048]{2,1,0:T(8,128)(2,1)}, u32[]{:S(2)}, u32[]{:S(2)}) collective-permute-start(bf16[1,768,2048]{2,1,0:T(8,128)(2,1)S(1)} %collective-permute-done), channel_id=1, source_target_pairs={{0,4},{4,8},{8,12},{12,16},{16,20},{20,24},{24,28},{28,32},{32,36}... | collective-permute-start | bytes 9437192 | tf_op jit(solution)/shard_map/ppermute | solution.py:11
  143.7 70.8 %collective-permute-start.2 = (bf16[1,768,2048]{2,1,0:T(8,128)(2,1)}, bf16[1,768,2048]{2,1,0:T(8,128)(2,1)}, u32[]{:S(2)}, u32[]{:S(2)}) collective-permute-start(bf16[1,768,2048]{2,1,0:T(8,128)(2,1)} %collective-permute-done.1), channel_id=1, source_target_pairs={{0,4},{4,8},{8,12},{12,16},{16,20},{20,24},{24,28},{28,32},{32,36}... | collective-permute-start | bytes 9437192 | tf_op jit(solution)/shard_map/ppermute | solution.py:11
  143.7 77.6 %copy-start.6 = (f32[256]{0:T(256)S(1)}, f32[256]{0:T(256)}, u32[]{:S(2)}) copy-start(f32[256]{0:T(256)} %param.9) | copy-start | bytes 3076
  143.7 77.6 %copy-start.7 = (s32[64]{0:T(128)S(1)}, s32[64]{0:T(128)}, u32[]{:S(2)}) copy-start(s32[64]{0:T(128)} %param.7) | copy-start | bytes 772
  143.7 78.4 %copy-start.4 = (s32[768]{0:T(1024)S(1)}, s32[768]{0:T(1024)}, u32[]{:S(2)}) copy-start(s32[768]{0:T(1024)} %param.8) | copy-start | bytes 9220
  143.7 78.4 %copy-start.5 = (f32[256]{0:T(256)S(1)}, f32[256]{0:T(256)}, u32[]{:S(2)}) copy-start(f32[256]{0:T(256)} %param.10) | copy-start | bytes 3076
  218.6 139.8 %collective-permute-start.3 = (bf16[1,768,2048]{2,1,0:T(8,128)(2,1)}, bf16[1,768,2048]{2,1,0:T(8,128)(2,1)}, u32[]{:S(2)}, u32[]{:S(2)}) collective-permute-start(bf16[1,768,2048]{2,1,0:T(8,128)(2,1)} %select_select_fusion), channel_id=1, source_target_pairs={{0,16},{4,20},{8,24},{12,28},{16,32},{20,36},{24,40},{28,44},{32,4... | collective-permute-start | bytes 9437192 | tf_op jit(solution)/shard_map/ppermute | solution.py:11
  368.5 8.3 %copy-start.2 = (f32[768,768]{1,0:T(8,128)S(1)}, f32[768,768]{1,0:T(8,128)}, u32[]{:S(2)}) copy-start(f32[768,768]{1,0:T(8,128)} %fusion.5) | copy-start | bytes 7077892
  368.5 8.3 %copy-start.3 = (f32[768,768]{0,1:T(8,128)S(1)}, f32[768,768]{0,1:T(8,128)}, u32[]{:S(2)}) copy-start(f32[768,768]{0,1:T(8,128)} %copy.14) | copy-start | bytes 7077892
where the time goes:
time: 575 us; the launch traced here: 574 us
  waiting for transfers between devices  335 us (58%)
  blocking collectives  184 us (32%)
  matrix products  31 us (5%)
  local copies, waits for them, and re-layouts  13.1 us (2%)
  starting transfers between devices  6.48 us (1%)
    ppermute x4, waiting for transfers between devices, passed_along(): lax.ppermute(value, axis, [(i, (i + by) % length) for i in range(length)])  335 us
    psum x1, blocking collectives, body(): total = lax.psum(blocks, 'off')  112 us
    all_to_all x1, blocking collectives, body(): lax.all_to_all(finished_flag[None], 'occ', split_axis=1, concat_axis=0, t...  72.3 us
    dot_general x2, matrix products, body(): lax.dot_general(other, pair_weight, (((0,), (1,)), ((), ())), preferred_e...  15 us
    dot_general x2, matrix products, body(): lax.dot_general(own, other, (((1,), (1,)), ((), ())), preferred_element_t...  13.9 us
  transfers between devices with their start and end apart: 4, of which 4 were waited for; matrix products, arithmetic and copies ran while one was open for 2% of the time, Pallas kernels for 0%

commit v1 on v0

--- a/solution.py
+++ b/solution.py
@@ -1,9 +1,17 @@
+import functools
 import jax
 import jax.numpy as jnp
 from jax import lax
 from jax.sharding import PartitionSpec as P
 
 PAIR_STEPS = 2
+
+
+def cut_the_point(point, comm_axis):
+    return jnp.sum(lax.all_gather(point, comm_axis), axis=0)
+
+
+pack_field = functools.partial(cut_the_point, comm_axis="off")
 
 
 def passed_along(value, axis, by):
@@ -52,7 +60,7 @@
     naux_rows = gamma.shape[0]
     per_device = naux_rows // (occ_count * off_count)
     blocks = gamma.reshape(occ_count, off_count, per_device, gamma.shape[1])
-    total = lax.psum(blocks, "off")
+    total = pack_field(blocks)
     mine = lax.dynamic_slice_in_dim(total, off_index, 1, 1)
     lower_gamma_part = mine.reshape(occ_count, per_device, gamma.shape[1]).astype(jnp.bfloat16)
     finished_flag = jnp.einsum(

time: 575 us -> 715 us (1.24)
  waiting for transfers between devices: 335 us -> 567 us
  blocking collectives: 184 us -> 66.4 us
  between operations: 0.08 us -> 13.5 us
  other arithmetic: 4.54 us -> 16.9 us
    all_gather x0 -> x1, waiting for transfers between devices: none -> 232 us  [cut_the_point(): return jnp.sum(lax.all_gather(point, comm_axis), axis=0)]
    psum x1 -> x0, blocking collectives: 112 us -> none  [body(): total = lax.psum(blocks, 'off')]
    reduce_sum x0 -> x1, other arithmetic: none -> 12.4 us  [cut_the_point(): return jnp.sum(lax.all_gather(point, comm_axis), axis=0)]
  transfers between devices with their start and end apart: 4 -> 5, of which waited for: 4 -> 5; matrix products, arithmetic and copies ran while one was open for 2% -> 2% of each run, Pallas kernels for 0% -> 0%
where the time goes in v1:
time: 715 us; the launch traced here: 714 us
  waiting for transfers between devices  567 us (79%)
  blocking collectives  66.4 us (9%)
  matrix products  33.9 us (5%)
  other arithmetic  16.9 us (2%)
  between operations  13.5 us (2%)
  local copies, waits for them, and re-layouts  9.8 us (1%)
    ppermute x4, waiting for transfers between devices, passed_along(): lax.ppermute(value, axis, [(i, (i + by) % length) for i in range(length)])  335 us
    all_gather x1, waiting for transfers between devices, cut_the_point(): return jnp.sum(lax.all_gather(point, comm_axis), axis=0)  232 us
    all_to_all x1, blocking collectives, body(): lax.all_to_all(finished_flag[None], 'occ', split_axis=1, concat_axis=0, t...  66.4 us
    dot_general x2, matrix products, body(): lax.dot_general(other, pair_weight, (((0,), (1,)), ((), ())), preferred_e...  17.8 us
  transfers between devices with their start and end apart: 5, of which 5 were waited for; matrix products, arithmetic and copies ran while one was open for 2% of the time, Pallas kernels for 0%

profile of v1, /device:TPU:56, one launch (start us, length us, event | category | flops | bytes accessed | tf_op | source)
XLA Modules:
  0.0 713.6 jit_solution(6589051798578993189)
XLA Ops:
  6.5 0.0 copy-start
  6.5 0.0 all-gather.2.cloned.1.call-start
  6.5 1.9 collective-permute-start
  8.5 68.1 %collective-permute-done = bf16[1,768,2048]{2,1,0:T(8,128)(2,1)S(1)} collective-permute-done((bf16[1,768,2048]{2,1,0:T(8,128)(2,1)}, bf16[1,768,2048]{2,1,0:T(8,128)(2,1)S(1)}, u32[]{:S(2)}, u32[]{:S(2)}) %collective-permute-start) | collective-permute-done | bytes 3145760 | tf_op jit(solution)/shard_map/ppermute | solution.py:19
  76.6 1.6 copy-done.1
  78.2 1.9 collective-permute-start.1
  80.2 70.1 %collective-permute-done.1 = bf16[1,768,2048]{2,1,0:T(8,128)(2,1)} collective-permute-done((bf16[1,768,2048]{2,1,0:T(8,128)(2,1)S(1)}, bf16[1,768,2048]{2,1,0:T(8,128)(2,1)}, u32[]{:S(2)}, u32[]{:S(2)}) %collective-permute-start.1) | collective-permute-done | bytes 3145760 | tf_op jit(solution)/shard_map/ppermute | solution.py:19
  150.3 0.0 collective-permute-start.2
  150.3 0.0 copy-start.5
  150.3 70.8 %collective-permute-done.2 = bf16[1,768,2048]{2,1,0:T(8,128)(2,1)} collective-permute-done((bf16[1,768,2048]{2,1,0:T(8,128)(2,1)}, bf16[1,768,2048]{2,1,0:T(8,128)(2,1)}, u32[]{:S(2)}, u32[]{:S(2)}) %collective-permute-start.2) | collective-permute-done | bytes 3145760 | tf_op jit(solution)/shard_map/ppermute | solution.py:19
  221.1 4.1 select_select_fusion
  225.2 2.6 collective-permute-start.3
  227.8 0.0 copy-done.6
  227.8 0.0 copy-done.7
  227.8 0.2 select_reduce_fusion.1
  228.0 0.6 fusion.33
  228.6 0.3 select_reduce_fusion
  228.9 6.9 fusion.5
  235.9 3.1 copy.13
  239.0 126.0 %collective-permute-done.3 = bf16[1,768,2048]{2,1,0:T(8,128)(2,1)} collective-permute-done((bf16[1,768,2048]{2,1,0:T(8,128)(2,1)}, bf16[1,768,2048]{2,1,0:T(8,128)(2,1)}, u32[]{:S(2)}, u32[]{:S(2)}) %collective-permute-start.3) | collective-permute-done | bytes 3145760 | tf_op jit(solution)/shard_map/ppermute | solution.py:19
  365.0 7.0 fusion.2
  372.0 3.1 copy.14
  375.1 8.3 %fusion = f32[2048,768]{1,0:T(8,128)S(1)} fusion(bf16[1,768,2048]{2,1,0:T(8,128)(2,1)} %collective-permute-done.3, f32[768,768]{0,1:T(8,128)} %copy.14, f32[768,768]{1,0:T(8,128)} %fusion.2, f32[]{:T(128)} %bitcast.7, f32[]{:T(128)} %bitcast.3, f32[768]{0:T(1024)S(1)} %select_reduce_fusion), kind=kOutput, calls=%fused_computation.1 | convolution fusion | flops 2420637696 | bytes 14158856 | tf_op jit(solution)/shard_map/dot_general | solution.py:57
  383.4 0.0 copy-done.2
  383.4 0.0 copy-done.3
  383.4 9.5 %convolution_add_fusion = f32[2048,768]{1,0:T(8,128)} fusion(f32[2048,768]{1,0:T(8,128)S(1)} %fusion, bf16[1,768,2048]{2,1,0:T(8,128)(2,1)} %select_select_fusion, f32[768,768]{0,1:T(8,128)S(1)} %copy-done.3, f32[768,768]{1,0:T(8,128)S(1)} %copy-done.2, f32[]{:T(128)} %bitcast.4, f32[]{:T(128)} %bitcast.3, f32[768]{0:T(1024)S(1)} %select_reduce_fusion), kind=kOutput, calls=%fused_computation | convolution fusion | flops 2422210560 | bytes 20450312 | tf_op jit(solution)/shard_map/dot_general | solution.py:57
  392.9 0.0 all-gather.2.cloned.1.call-update
  392.9 231.6 %all-gather.2.cloned.1.call-done = f32[4,64,4,8,768]{4,3,2,1,0:T(8,128)} async-done(((f32[1,64,4,8,768]{4,3,2,1,0:T(8,128)}), f32[4,64,4,8,768]{4,3,2,1,0:T(8,128)}) %all-gather.2.cloned.1.call-update) | async-done | bytes 25165840 | tf_op jit(solution)/shard_map/all_gather | solution.py:11
  624.5 12.4 %reduce_sum.29 = bf16[64,4,8,768]{3,2,1,0:T(8,128)(2,1)} reduce(f32[4,64,4,8,768]{4,3,2,1,0:T(8,128)} %all-gather.2.cloned.1.call-done, f32[]{:T(128)} %constant.39.clone.1), dimensions={0}, to_apply=%region_2.3 | reduce | flops 4718592 | bytes 28311556 | tf_op jit(solution)/shard_map/reduce_sum | solution.py:11
  636.9 2.1 convolution_bitcast_fusion
  639.0 66.4 %all_to_all.4 = f32[1,64,8,1024]{3,2,0,1:T(8,128)S(1)} all-to-all(f32[1,64,8,1024]{3,2,0,1:T(8,128)S(1)} %convolution_bitcast_fusion), channel_id=1, replica_groups=mesh['occ'=64,'off'=4] {'occ'}, dimensions={1} | all-to-all | bytes 4194304 | tf_op jit(solution)/shard_map/all_to_all | solution.py:72
  705.4 1.3 copy.19
  (9 shorter events, 0.0 us)
Async XLA Ops:
  6.5 630.4 %copy-start = (bf16[768,1024]{1,0:T(8,128)(2,1)S(1)}, bf16[768,1024]{1,0:T(8,128)(2,1)}, u32[]{:S(2)}) copy-start(bf16[768,1024]{1,0:T(8,128)(2,1)} %param.11) | copy-start | bytes 4718596
  6.5 618.0 %all-gather.2.cloned.1.call-start = ((), (), s32[]{:S(2)}) async-start(), calls=%async_computation.1 | async-start | bytes 31457280 | tf_op jit(solution)/shard_map/all_gather | solution.py:11
  6.5 70.1 %collective-permute-start = (bf16[1,768,2048]{2,1,0:T(8,128)(2,1)}, bf16[1,768,2048]{2,1,0:T(8,128)(2,1)S(1)}, u32[]{:S(2)}, u32[]{:S(2)}) collective-permute-start(bf16[1,768,2048]{2,1,0:T(8,128)(2,1)} %param.6), channel_id=1, source_target_pairs={{0,4},{4,8},{8,12},{12,16},{16,20},{20,24},{24,28},{28,32},{32,36}... | collective-permute-start | bytes 9437192 | tf_op jit(solution)/shard_map/ppermute | solution.py:19
  76.6 1.7 copy-start.1
  78.2 72.0 %collective-permute-start.1 = (bf16[1,768,2048]{2,1,0:T(8,128)(2,1)S(1)}, bf16[1,768,2048]{2,1,0:T(8,128)(2,1)}, u32[]{:S(2)}, u32[]{:S(2)}) collective-permute-start(bf16[1,768,2048]{2,1,0:T(8,128)(2,1)S(1)} %collective-permute-done), channel_id=1, source_target_pairs={{0,4},{4,8},{8,12},{12,16},{16,20},{20,24},{24,28},{28,32},{32,36}... | collective-permute-start | bytes 9437192 | tf_op jit(solution)/shard_map/ppermute | solution.py:19
  150.3 70.8 %collective-permute-start.2 = (bf16[1,768,2048]{2,1,0:T(8,128)(2,1)}, bf16[1,768,2048]{2,1,0:T(8,128)(2,1)}, u32[]{:S(2)}, u32[]{:S(2)}) collective-permute-start(bf16[1,768,2048]{2,1,0:T(8,128)(2,1)} %collective-permute-done.1), channel_id=1, source_target_pairs={{0,4},{4,8},{8,12},{12,16},{16,20},{20,24},{24,28},{28,32},{32,36}... | collective-permute-start | bytes 9437192 | tf_op jit(solution)/shard_map/ppermute | solution.py:19
  150.3 77.6 %copy-start.6 = (f32[256]{0:T(256)S(1)}, f32[256]{0:T(256)}, u32[]{:S(2)}) copy-start(f32[256]{0:T(256)} %param.9) | copy-start | bytes 3076
  150.3 77.6 %copy-start.7 = (s32[64]{0:T(128)S(1)}, s32[64]{0:T(128)}, u32[]{:S(2)}) copy-start(s32[64]{0:T(128)} %param.7) | copy-start | bytes 772
  150.3 78.4 %copy-start.4 = (s32[768]{0:T(1024)S(1)}, s32[768]{0:T(1024)}, u32[]{:S(2)}) copy-start(s32[768]{0:T(1024)} %param.8) | copy-start | bytes 9220
  150.3 78.4 %copy-start.5 = (f32[256]{0:T(256)S(1)}, f32[256]{0:T(256)}, u32[]{:S(2)}) copy-start(f32[256]{0:T(256)} %param.10) | copy-start | bytes 3076
  225.2 139.8 %collective-permute-start.3 = (bf16[1,768,2048]{2,1,0:T(8,128)(2,1)}, bf16[1,768,2048]{2,1,0:T(8,128)(2,1)}, u32[]{:S(2)}, u32[]{:S(2)}) collective-permute-start(bf16[1,768,2048]{2,1,0:T(8,128)(2,1)} %select_select_fusion), channel_id=1, source_target_pairs={{0,16},{4,20},{8,24},{12,28},{16,32},{20,36},{24,40},{28,44},{32,4... | collective-permute-start | bytes 9437192 | tf_op jit(solution)/shard_map/ppermute | solution.py:19
  375.1 8.3 %copy-start.2 = (f32[768,768]{1,0:T(8,128)S(1)}, f32[768,768]{1,0:T(8,128)}, u32[]{:S(2)}) copy-start(f32[768,768]{1,0:T(8,128)} %fusion.5) | copy-start | bytes 7077892
  375.1 8.3 %copy-start.3 = (f32[768,768]{0,1:T(8,128)S(1)}, f32[768,768]{0,1:T(8,128)}, u32[]{:S(2)}) copy-start(f32[768,768]{0,1:T(8,128)} %copy.13) | copy-start | bytes 7077892
Sparse Core Ops, SparseCore 0:
  393.1 231.4 all-gather.1
